TPU v7x, 256 devices: a whole 4x4x8 slice. The times are simulated.
256 devices in a mesh: fsdp: 32 (over z, x_hi, core), tensor: 8 (over x_lo, y).
Axes of the slice: x: 4 (x_hi: 2, x_lo: 2; x = x_hi * 2 + x_lo), y: 4, z: 8, core: 2. Of those that a mesh axis runs over, the one named last changes fastest.
Arguments:
- tokens: bfloat16 [49152, 8192], P(('fsdp', 'tensor'))
- gain: bfloat16 [8192], replicated, may hold values from 0.5 to 1.5
- kv_weight: bfloat16 [8192, 2048], P('fsdp', 'tensor'), may hold values from -0.09375 to 0.09375
- block_mask: int32 [64, 16], P('fsdp', 'tensor'), may hold values from 0 to 1
- cotangent: bfloat16 [49152, 2048], P('fsdp', 'tensor'), may hold values from -0.02734375 to 0.02734375
Outputs:
- projected: bfloat16 [49152, 2048], P('fsdp', 'tensor')
- weight_grad: float32 [8192, 2048], P('fsdp', 'tensor')
All inputs are finite; a program needn't handle non-finite values.
Results may differ from a plain program's by a relative error of at most 0.005.
Values may be sent and summed in bfloat16 or wider, within the bound.
A program may use at most 128 MiB of HBM per device.

v0:
```python
import jax
import jax.numpy as jnp
from jax import lax
from jax.sharding import PartitionSpec as P


def normalize(rows, gain):
    values = rows.astype(jnp.float32)
    square = jnp.mean(values * values, axis=-1, keepdims=True)
    return (values * lax.rsqrt(square + 1e-05) * gain.astype(jnp.float32)).astype(jnp.bfloat16)


def apply_mask(panel, mask):
    rows, cols = panel.shape
    mrows, mcols = mask.shape
    shaped = panel.reshape(mrows, rows // mrows, mcols, cols // mcols)
    kept = shaped * mask[:, None, :, None].astype(panel.dtype)
    return kept.reshape(rows, cols)


def per_device(tokens, gain, kv_weight, block_mask, cotangent):
    group = lax.all_gather(normalize(tokens, gain), "tensor", axis=0, tiled=True)
    columns = group
    total = jnp.dot(
        columns,
        apply_mask(
            lax.all_gather(kv_weight, "fsdp", axis=0, tiled=True),
            lax.all_gather(block_mask, "fsdp", axis=0, tiled=True),
        ),
        preferred_element_type=jnp.float32,
    )
    projected = total.astype(jnp.bfloat16)
    columns = group
    summed = lax.psum_scatter(
        lax.dot_general(
            columns, cotangent, (((0,), (0,)), ((), ())), preferred_element_type=jnp.float32
        ),
        "fsdp",
        scatter_dimension=0,
        tiled=True,
    )
    weight_grad = apply_mask(summed, block_mask)
    return (projected, weight_grad)


def solution(mesh):
    return jax.shard_map(
        per_device,
        mesh=mesh,
        in_specs=(
            P(("fsdp", "tensor"), None),
            P(),
            P("fsdp", "tensor"),
            P("fsdp", "tensor"),
            P("fsdp", "tensor"),
        ),
        out_specs=(P("fsdp", "tensor"), P("fsdp", "tensor")),
        check_vma=False,
    )
```

profile of v0, /device:TPU:8, one launch (start us, length us, event | category | flops | bytes accessed | tf_op | source)
XLA Modules:
  0.0 521.2 jit_solution(9037868814021527761)
XLA Ops:
  7.2 0.0 copy-start
  7.2 0.0 all-gather.4.cloned.1.call-start
  7.2 0.8 convert_element_type.21
  8.0 2.6 fusion
  10.6 4.5 fusion.2
  15.1 0.0 all-gather.4.cloned.1.call-update
  15.1 0.0 all-gather.6.cloned.1.call-start
  15.2 0.7 all-gather.6.cloned.1.call-update
  15.9 0.0 reduce-scatter.2.cloned.1.call-start
  15.9 251.8 %all-gather.4.cloned.1.call-done = bf16[1536,8192]{1,0:T(8,128)(2,1)} async-done(((bf16[192,8192]{1,0:T(8,128)(2,1)}), bf16[1536,8192]{1,0:T(8,128)(2,1)}) %all-gather.4.cloned.1.call-update) | async-done | bytes 25165840 | tf_op jit(solution)/shard_map/all_gather | solution.py:22
  267.7 0.0 copy-done
  267.7 13.9 %fusion.6 = f32[8192,256]{1,0:T(8,128)} fusion(bf16[1536,8192]{1,0:T(8,128)(2,1)} %all-gather.4.cloned.1.call-done, bf16[1536,256]{1,0:T(8,128)(2,1)S(1)} %copy-done), kind=kOutput, calls=%fused_computation.11 | convolution fusion | flops 6442450944 | bytes 34340864 | tf_op jit(solution)/shard_map/dot_general | solution.py:35
  281.7 0.0 copy-start.1
  281.7 0.0 reduce-scatter.2.cloned.1.call-update
  281.7 0.7 copy-done.1
  282.4 42.1 %all-gather = s32[32,2,2]{2,1,0:T(2,128)S(1)} all-gather(s32[1,2,2]{2,1,0:T(2,128)S(1)} %bitcast.19), channel_id=1, replica_groups=mesh['fsdp'=32,'tensor'=8] {'fsdp'}, dimensions={0}, use_global_device_ids=true | all-gather | bytes 528 | tf_op jit(solution)/shard_map/all_gather | solution.py:28
  324.5 0.1 copy.13
  324.6 0.1 copy.16
  324.7 33.6 %all-gather.6.cloned.1.call-done = bf16[8192,256]{1,0:T(8,128)(2,1)} async-done(((bf16[256,256]{1,0:T(8,128)(2,1)}), bf16[8192,256]{1,0:T(8,128)(2,1)}) %all-gather.6.cloned.1.call-update) | async-done | bytes 4194320 | tf_op jit(solution)/shard_map/all_gather | solution.py:27
  358.3 2.2 mul.46
  360.5 13.5 %fusion.5 = bf16[1536,256]{1,0:T(8,128)(2,1)} fusion(bf16[1536,8192]{1,0:T(8,128)(2,1)} %all-gather.4.cloned.1.call-done, bf16[8192,256]{1,0:T(8,128)(2,1)} %all-gather.6.cloned.1.call-done, bf16[1024,8,2,128]{3,2,1,0:T(2,128)(2,1)S(1)} %bitcast.16), kind=kOutput, calls=%fused_computation.8 | convolution fusion | flops 6444941312 | bytes 34340864 | tf_op jit(solution)/shard_map/dot_general | solution.py:24
  374.1 138.8 %reduce-scatter.2.cloned.1.call-done = f32[256,256]{1,0:T(8,128)} async-done(((f32[8192,256]{1,0:T(8,128)}), f32[256,256]{1,0:T(8,128)}) %reduce-scatter.2.cloned.1.call-update) | async-done | bytes 262160 | tf_op jit(solution)/shard_map/reduce_scatter | solution.py:34
  512.9 0.1 mul.49
  513.0 1.7 bitcast_multiply_fusion.4
  (3 shorter events, 0.0 us)
Async XLA Ops:
  7.2 260.6 %copy-start = (bf16[1536,256]{1,0:T(8,128)(2,1)S(1)}, bf16[1536,256]{1,0:T(8,128)(2,1)}, u32[]{:S(2)}) copy-start(bf16[1536,256]{1,0:T(8,128)(2,1)} %param.9) | copy-start | bytes 2359300
  7.2 260.6 %all-gather.4.cloned.1.call-start = ((), (), s32[]{:S(2)}) async-start(), calls=%async_computation.1 | async-start | bytes 28311552 | tf_op jit(solution)/shard_map/all_gather | solution.py:22
  15.1 343.2 %all-gather.6.cloned.1.call-start = ((), (), s32[]{:S(2)}) async-start(), calls=%async_computation.2 | async-start | bytes 4325376 | tf_op jit(solution)/shard_map/all_gather | solution.py:27
  15.9 497.0 %reduce-scatter.2.cloned.1.call-start = ((), (), s32[]{:S(2)}) async-start(), calls=%async_computation.3 | async-start | bytes 8650752 | tf_op jit(solution)/shard_map/reduce_scatter | solution.py:34
  281.7 0.7 copy-start.1
Sparse Core Ops, SparseCore 0:
  15.2 252.4 all-gather.3
  270.5 87.7 all-gather.5
  362.7 150.0 reduce-scatter.1
where the time goes:
time: 521 us
  waiting for transfers between devices  425 us (82%)
  blocking collectives  42.1 us (8%)
  matrix products  27.5 us (5%)
  between operations  13.8 us (3%)
  other arithmetic  9.57 us (2%)
    all_gather x1, waiting for transfers between devices, per_device(): lax.all_gather(normalize(tokens, gain), 'tensor', axis=0, tiled=True)  252 us
    reduce_scatter x1, waiting for transfers between devices, per_device(): lax.psum_scatter(lax.dot_general(columns, cotangent, (((0,), (0,)), ((),...  139 us
    all_gather x1, blocking collectives, per_device(): lax.all_gather(block_mask, 'fsdp', axis=0, tiled=True)  42.1 us
    all_gather x1, waiting for transfers between devices, per_device(): lax.all_gather(kv_weight, 'fsdp', axis=0, tiled=True)  33.6 us
    dot_general x1, matrix products, per_device(): lax.dot_general(columns, cotangent, (((0,), (0,)), ((), ())), preferred_e...  13.9 us
    dot_general x1, matrix products, per_device(): jnp.dot(columns, apply_mask(lax.all_gather(kv_weight, 'fsdp', axis=0, til...  13.5 us
  transfers between devices with their start and end apart: 3, of which 3 were waited for; matrix products, arithmetic and copies ran while one was open for 6% of the time, Pallas kernels for 0%

commit v1 on v0

--- a/solution.py
+++ b/solution.py
@@ -24,7 +24,9 @@
     total = jnp.dot(
         columns,
         apply_mask(
-            lax.all_gather(kv_weight, "fsdp", axis=0, tiled=True),
+            jnp.concatenate(
+                lax.all_to_all(jnp.stack([kv_weight] * lax.axis_size("fsdp")), "fsdp", 0, 0), axis=0
+            ),
             lax.all_gather(block_mask, "fsdp", axis=0, tiled=True),
         ),
         preferred_element_type=jnp.float32,

time: 521 us -> 478 us (0.917)
  waiting for transfers between devices: 425 us -> 267 us
  blocking collectives: 42.1 us -> 144 us
  starting transfers between devices: 0.12 us -> 10 us
    reduce_scatter x1, waiting for transfers between devices: 139 us -> 14.6 us  [per_device(): lax.psum_scatter(lax.dot_general(columns, cotangent, (((0,), (0,)), ((),...]
    all_gather x1, blocking collectives: 42.1 us -> 144 us  [per_device(): lax.all_gather(block_mask, 'fsdp', axis=0, tiled=True)]
    all_gather x1 -> x0, waiting for transfers between devices: 33.6 us -> none  [per_device(): lax.all_gather(kv_weight, 'fsdp', axis=0, tiled=True)]
    all_to_all x0 -> x1, starting transfers between devices: none -> 9.95 us  [per_device(): lax.all_to_all(jnp.stack([kv_weight] * lax.axis_size('fsdp')), 'fsdp', 0, 0)]
  transfers between devices with their start and end apart: 3 -> 3, of which waited for: 3 -> 2; matrix products, arithmetic and copies ran while one was open for 6% -> 4% of each run, Pallas kernels for 0% -> 0%
where the time goes in v1:
time: 478 us
  waiting for transfers between devices  267 us (56%)
  blocking collectives  144 us (30%)
  matrix products  27.5 us (6%)
  between operations  14.1 us (3%)
  starting transfers between devices  10 us (2%)
  other arithmetic  9.57 us (2%)
  local copies, waits for them, and re-layouts  5.88 us (1%)
    all_gather x1, waiting for transfers between devices, per_device(): lax.all_gather(normalize(tokens, gain), 'tensor', axis=0, tiled=True)  253 us
    all_gather x1, blocking collectives, per_device(): lax.all_gather(block_mask, 'fsdp', axis=0, tiled=True)  144 us
    reduce_scatter x1, waiting for transfers between devices, per_device(): lax.psum_scatter(lax.dot_general(columns, cotangent, (((0,), (0,)), ((),...  14.6 us
    dot_general x1, matrix products, per_device(): lax.dot_general(columns, cotangent, (((0,), (0,)), ((), ())), preferred_e...  13.9 us
    dot_general x1, matrix products, per_device(): jnp.dot(columns, apply_mask(jnp.concatenate(lax.all_to_all(jnp.stack([kv_...  13.6 us
    all_to_all x1, starting transfers between devices, per_device(): lax.all_to_all(jnp.stack([kv_weight] * lax.axis_size('fsdp')), 'fsdp', 0, 0)  9.95 us
  transfers between devices with their start and end apart: 3, of which 2 were waited for; matrix products, arithmetic and copies ran while one was open for 4% of the time, Pallas kernels for 0%

profile of v1, /device:TPU:8, one launch (start us, length us, event | category | flops | bytes accessed | tf_op | source)
XLA Modules:
  0.0 478.1 jit_solution(15599427118751205558)
XLA Ops:
  7.2 0.0 copy-start
  7.2 0.0 all-gather.3.cloned.1.call-start
  7.2 0.8 convert_element_type.21
  8.0 2.6 fusion
  10.6 4.5 fusion.2
  15.1 0.0 all-gather.3.cloned.1.call-update
  15.1 0.0 reduce-scatter.2.cloned.1.call-start
  15.2 252.6 %all-gather.3.cloned.1.call-done = bf16[1536,8192]{1,0:T(8,128)(2,1)} async-done(((bf16[192,8192]{1,0:T(8,128)(2,1)}), bf16[1536,8192]{1,0:T(8,128)(2,1)}) %all-gather.3.cloned.1.call-update) | async-done | bytes 25165840 | tf_op jit(solution)/shard_map/all_gather | solution.py:22
  267.7 0.0 copy-done
  267.7 13.9 %fusion.6 = f32[8192,256]{1,0:T(8,128)} fusion(bf16[1536,8192]{1,0:T(8,128)(2,1)} %all-gather.3.cloned.1.call-done, bf16[1536,256]{1,0:T(8,128)(2,1)S(1)} %copy-done), kind=kOutput, calls=%fused_computation.11 | convolution fusion | flops 6442450944 | bytes 34340864 | tf_op jit(solution)/shard_map/dot_general | solution.py:37
  281.7 0.0 copy-start.1
  281.7 0.0 reduce-scatter.2.cloned.1.call-update
  281.7 0.9 copy-done.1
  282.6 0.0 copy-start.2
  282.6 2.4 stack.2
  285.0 9.9 %all-to-all-start = ((bf16[32,256,256]{2,1,0:T(8,128)(2,1)}), bf16[32,256,256]{2,1,0:T(8,128)(2,1)}, u32[]{:S(2)}, u32[]{:S(2)}) async-start(bf16[32,256,256]{2,1,0:T(8,128)(2,1)} %stack.2), calls=%async_computation | async-start | bytes 8388608 | tf_op jit(solution)/shard_map/all_to_all | solution.py:28
  295.0 0.0 copy-done.2
  295.0 143.8 %all-gather = s32[32,2,2]{2,1,0:T(2,128)S(1)} all-gather(s32[1,2,2]{2,1,0:T(2,128)S(1)} %bitcast.20), channel_id=1, replica_groups=mesh['fsdp'=32,'tensor'=8] {'fsdp'}, dimensions={0}, use_global_device_ids=true | all-gather | bytes 528 | tf_op jit(solution)/shard_map/all_gather | solution.py:30
  438.8 0.1 copy.13
  438.9 0.1 copy.16
  439.0 0.0 all-to-all-done
  439.0 2.2 mul.46
  441.3 13.6 %fusion.5 = bf16[1536,256]{1,0:T(8,128)(2,1)} fusion(bf16[1536,8192]{1,0:T(8,128)(2,1)} %all-gather.3.cloned.1.call-done, bf16[8192,256]{1,0:T(8,128)(2,1)} %bitcast, bf16[1024,8,2,128]{3,2,1,0:T(2,128)(2,1)S(1)} %bitcast.17), kind=kOutput, calls=%fused_computation.8 | convolution fusion | flops 6444941312 | bytes 34340864 | tf_op jit(solution)/shard_map/dot_general | solution.py:24
  454.9 14.6 %reduce-scatter.2.cloned.1.call-done = f32[256,256]{1,0:T(8,128)} async-done(((f32[8192,256]{1,0:T(8,128)}), f32[256,256]{1,0:T(8,128)}) %reduce-scatter.2.cloned.1.call-update) | async-done | bytes 262160 | tf_op jit(solution)/shard_map/reduce_scatter | solution.py:36
  469.4 0.1 mul.49
  469.6 1.7 bitcast_multiply_fusion.4
  (3 shorter events, 0.0 us)
Async XLA Ops:
  7.2 260.6 %copy-start = (bf16[1536,256]{1,0:T(8,128)(2,1)S(1)}, bf16[1536,256]{1,0:T(8,128)(2,1)}, u32[]{:S(2)}) copy-start(bf16[1536,256]{1,0:T(8,128)(2,1)} %param.9) | copy-start | bytes 2359300
  7.2 260.6 %all-gather.3.cloned.1.call-start = ((), (), s32[]{:S(2)}) async-start(), calls=%async_computation.2 | async-start | bytes 28311552 | tf_op jit(solution)/shard_map/all_gather | solution.py:22
  15.1 454.3 %reduce-scatter.2.cloned.1.call-start = ((), (), s32[]{:S(2)}) async-start(), calls=%async_computation.3 | async-start | bytes 8650752 | tf_op jit(solution)/shard_map/reduce_scatter | solution.py:36
  281.7 0.9 copy-start.1
  282.6 12.4 %copy-start.2 = (s32[2,2]{1,0:T(2,128)S(1)}, s32[2,2]{1,0:T(2,128)}, u32[]{:S(2)}) copy-start(s32[2,2]{1,0:T(2,128)} %param.8) | copy-start | bytes 52
  285.0 154.0 %all-to-all-start = ((bf16[32,256,256]{2,1,0:T(8,128)(2,1)}), bf16[32,256,256]{2,1,0:T(8,128)(2,1)}, u32[]{:S(2)}, u32[]{:S(2)}) async-start(bf16[32,256,256]{2,1,0:T(8,128)(2,1)} %stack.2), calls=%async_computation | async-start | bytes 8388608 | tf_op jit(solution)/shard_map/all_to_all | solution.py:28
Sparse Core Ops, SparseCore 0:
  15.2 252.4 all-gather.2
  281.8 187.5 reduce-scatter.1
